TPU v7x, 32 devices: a whole 2x2x4 slice. The times are simulated.
32 devices in a mesh: frame: 4 (over x, core), cam: 8 (over z, y).
Axes of the slice: x: 2, y: 2, z: 4, core: 2. Of those that a mesh axis runs over, the one named last changes fastest.
Arguments:
- view_maps: bfloat16 [8, 88, 2, 32, 256], P('frame', 'cam'), may hold values from -6 to 6
- conv_weight: bfloat16 [9, 256, 256], replicated, may hold values from -0.125 to 0.125
- join_weight: bfloat16 [16384, 256], P('cam'), may hold values from -0.1875 to 0.1875
- valid_cams: int32 [8, 88], P('frame'), may hold values from 0 to 1, as said below
- latent_grad: bfloat16 [8, 256], P('frame'), may hold values from -6 to 6
Outputs:
- latent: float32 [8, 256], P('frame')
- conv_grad: float32 [9, 256, 256], replicated
- join_grad: float32 [16384, 256], P(('cam', 'frame'))
Inputs may be any that keep to these rules, and one draw needn't show every extreme that they name: `valid_cams`: every frame has at least one usable camera; the last 6 cameras are padding and never usable.
All inputs are finite; a program needn't handle non-finite values.
Results may differ from a plain program's by a relative error of at most 0.007.
Values may be sent and summed in bfloat16 or wider, within the bound.
A program may use at most 64 MiB of HBM per device.

v0:
```python
import jax
import jax.numpy as jnp
from jax import lax
from jax.sharding import PartitionSpec as P


def make_shifts(maps, rows_n, cols_n, chans):
    padded = jnp.pad(maps, ((0, 0), (0, 0), (1, 1), (1, 1), (0, 0)))
    return [
        padded[:, :, dy : dy + rows_n, dx : dx + cols_n, :].reshape(-1, chans)
        for dy in range(3)
        for dx in range(3)
    ]


def on_device(view_maps, conv_weight, join_weight, valid_cams, latent_grad):
    frames_here, cams_here, rows_n, cols_n, chans = view_maps.shape
    feat_len = rows_n * cols_n * chans
    shifted = make_shifts(view_maps, rows_n, cols_n, chans)
    preact = jnp.zeros((frames_here * cams_here * rows_n * cols_n, chans), jnp.float32)
    for k in range(9):
        preact = preact + jnp.dot(shifted[k], conv_weight[k], preferred_element_type=jnp.float32)
    sigma = jax.nn.sigmoid(preact)
    features = (preact * sigma).astype(jnp.bfloat16)
    features = features.reshape(frames_here, cams_here, feat_len)
    slopes = (sigma * (1.0 + preact * (1.0 - sigma))).reshape(frames_here, cams_here, feat_len)
    cam_count = jnp.sum(valid_cams.astype(jnp.float32), axis=1)
    local_valid = lax.dynamic_slice_in_dim(
        valid_cams, lax.axis_index("cam") * cams_here, cams_here, 1
    )
    mask_f = local_valid.astype(jnp.float32)
    mask_b = local_valid.astype(jnp.bfloat16)
    share_len = feat_len // lax.axis_size("cam")
    pooled = lax.psum_scatter(
        jnp.einsum("fc,fcp->pf", mask_b, features, preferred_element_type=jnp.float32),
        "cam",
        scatter_dimension=0,
        tiled=True,
    )
    joined = (pooled.T / cam_count[:, None]).astype(jnp.bfloat16)
    partial_latent = jnp.dot(joined, join_weight, preferred_element_type=jnp.float32)
    latent = lax.psum(partial_latent, "cam")
    joined_grad = jnp.einsum(
        "fl,sl->fs", latent_grad, join_weight, preferred_element_type=jnp.float32
    ).astype(jnp.bfloat16)
    weighting = mask_f / cam_count[:, None]
    scaled = (
        lax.all_gather(joined_grad, "cam", axis=1, tiled=True).astype(jnp.float32)[:, None, :]
        * weighting[:, :, None]
        * slopes
    )
    pre_grad = scaled.astype(jnp.bfloat16)
    pre_grad = pre_grad.reshape(-1, chans)
    taps = jnp.stack(
        [
            lax.dot_general(
                shifted[k], pre_grad, (((0,), (0,)), ((), ())), preferred_element_type=jnp.float32
            )
            for k in range(9)
        ]
    )
    sub_len = share_len // lax.axis_size("frame")
    all_joined, all_cotangent = (
        lax.all_gather(joined, "frame", axis=0, tiled=True),
        lax.all_gather(latent_grad, "frame", axis=0, tiled=True),
    )
    own_rows = lax.dynamic_slice_in_dim(all_joined, lax.axis_index("frame") * sub_len, sub_len, 1)
    join_grad = lax.dot_general(
        own_rows, all_cotangent, (((0,), (0,)), ((), ())), preferred_element_type=jnp.float32
    )
    conv_grad = lax.psum(taps, ("frame", "cam"))
    return (latent, conv_grad, join_grad)


def solution(mesh):
    in_specs = (
        P("frame", "cam", None, None, None),
        P(),
        P("cam", None),
        P("frame", None),
        P("frame", None),
    )
    out_specs = (P("frame", None), P(), P(("cam", "frame"), None))
    return jax.shard_map(
        on_device, mesh=mesh, in_specs=in_specs, out_specs=out_specs, check_vma=False
    )
```

profile of v0, /device:TPU:0, one launch (start us, length us, event | category | flops | bytes accessed | tf_op | source)
XLA Modules:
  0.0 305.6 jit_solution(8454710060224463295)
XLA Ops:
  8.1 4.9 %pad_slice_fusion = (bf16[2,11,2,32,256]{4,3,2,1,0:T(8,128)(2,1)}, bf16[2,11,2,32,256]{4,3,2,1,0:T(8,128)(2,1)}, bf16[2,11,2,32,256]{4,3,2,1,0:T(8,128)(2,1)}, b...) fusion(bf16[2,11,2,32,256]{4,3,2,1,0:T(8,128)(2,1)} %param.5), kind=kLoop, calls=%fused_computation | loop fusion | bytes 6488064 | tf_op jit(solution)/shard_map/slice | solution.py:10
  13.7 32.4 %all_gather.9 = bf16[2,16384]{1,0:T(2,128)(2,1)S(1)} all-gather(bf16[2,2048]{1,0:T(2,128)(2,1)S(1)} %convolution_convert_fusion), channel_id=1, replica_groups=mesh['frame'=4,'cam'=8] {'cam'}, dimensions={1}, use_global_device_ids=true | all-gather | bytes 73728 | tf_op jit(solution)/shard_map/all_gather | solution.py:48
  46.3 1.4 mul.41
  47.7 1.6 fusion.17
  49.8 0.8 copy-done.9
  50.9 0.8 copy-done.7
  52.1 0.8 copy-done.1
  53.2 0.8 copy-done.5
  54.3 0.8 copy-done.3
  55.4 0.8 copy-done.2
  56.5 1.0 copy-done.14
  57.7 1.9 multiply_convert_fusion
  59.6 1.6 reshape.53
  61.6 4.9 %copy.14 = f32[16384,2]{1,0:T(8,128)} copy(f32[16384,2]{0,1:T(2,128)S(1)} %bitcast.140) | data formatting | bytes 262144
  66.6 1.0 copy-done.13
  67.6 2.3 fusion.8
  69.9 1.1 fusion.7
  71.0 1.1 fusion.6
  72.2 1.1 fusion.5
  73.3 1.1 fusion.4
  74.4 1.1 fusion.3
  75.5 1.1 fusion.2
  76.6 1.1 fusion.1
  77.7 1.1 fusion
  78.9 5.1 %all-gather.1 = bf16[4,2,256]{2,1,0:T(2,128)(2,1)S(1)} all-gather(bf16[1,2,256]{2,1,0:T(2,128)(2,1)S(1)} %bitcast.141), channel_id=1, replica_groups=mesh['frame'=4,'cam'=8] {'frame'}, dimensions={0}, use_global_device_ids=true | all-gather | bytes 5120 | tf_op jit(solution)/shard_map/all_gather | solution.py:65
  84.0 142.1 %reduce-scatter.4.cloned.1.call-done = f32[2048,2]{1,0:T(8,128)} async-done(((f32[16384,2]{1,0:T(8,128)}), f32[2048,2]{1,0:T(8,128)}) %reduce-scatter.4.cloned.1.call-update) | async-done | bytes 16400
  226.0 1.6 copy.15
  227.7 5.2 %all-gather = bf16[4,2,2048]{2,1,0:T(2,128)(2,1)S(1)} all-gather(bf16[1,2,2048]{2,1,0:T(2,128)(2,1)S(1)} %fusion.68), channel_id=1, replica_groups=mesh['frame'=4,'cam'=8] {'frame'}, dimensions={0}, use_global_device_ids=true | all-gather | bytes 40960 | tf_op jit(solution)/shard_map/all_gather | solution.py:64
  233.2 20.2 %psum.14 = f32[2,256]{1,0:T(2,128)} all-reduce(f32[2,256]{1,0:T(2,128)S(1)} %fusion.34), channel_id=1, replica_groups=mesh['frame'=4,'cam'=8] {'cam'}, use_global_device_ids=true, to_apply=%region_2.3 | all-reduce | flops 512 | bytes 4096 | tf_op jit(solution)/shard_map/psum | solution.py:42
  253.4 1.1 fusion.28
  254.4 40.5 %all-reduce.3.cloned.1.call-done = f32[9,256,256]{2,1,0:T(8,128)} async-done(((f32[9,256,256]{2,1,0:T(8,128)}), f32[9,256,256]{2,1,0:T(8,128)}) %all-reduce.3.cloned.1.call-update) | async-done | bytes 2359312 | tf_op jit(solution)/shard_map/psum | solution.py:71
  294.9 3.2 %copy.29 = f32[9,256,256]{2,1,0:T(8,128)} copy(f32[9,256,256]{2,1,0:T(8,128)} %all-reduce.3.cloned.1.call-done) | data formatting | bytes 4718592
  (57 shorter events, 4.6 us)
Async XLA Ops:
  8.0 5.3 %copy-start = (bf16[2048,256]{1,0:T(8,128)(2,1)S(1)}, bf16[2048,256]{1,0:T(8,128)(2,1)}, u32[]{:S(2)}) copy-start(bf16[2048,256]{1,0:T(8,128)(2,1)} %param.7) | copy-start | bytes 3145732
  8.0 218.0 %reduce-scatter.4.cloned.1.call-start = ((), (), s32[]{:S(2)}) async-start(), calls=%async_computation.2 | async-start | bytes 9437184
  8.1 5.0 %copy-start.20 = (s32[2,88]{1,0:T(2,128)S(1)}, s32[2,88]{1,0:T(2,128)}, u32[]{:S(2)}) copy-start(s32[2,88]{1,0:T(2,128)} %param.8) | copy-start | bytes 2116
  8.1 5.2 %copy-start.19 = (bf16[2,256]{1,0:T(2,128)(2,1)S(1)}, bf16[2,256]{1,0:T(2,128)(2,1)}, u32[]{:S(2)}) copy-start(bf16[2,256]{1,0:T(2,128)(2,1)} %param.9) | copy-start | bytes 3076
  47.7 1.6 copy-start.11
  47.7 1.7 copy-start.15
  49.5 1.1 copy-start.9
  50.6 1.1 copy-start.7
  51.7 1.1 copy-start.1
  52.8 1.1 copy-start.5
  53.9 1.1 copy-start.3
  55.0 1.1 copy-start.2
  56.1 1.4 copy-start.14
  56.1 1.5 copy-start.16
  66.5 1.1 copy-start.13
  66.5 228.4 %all-reduce.3.cloned.1.call-start = ((), (), s32[]{:S(2)}) async-start(), calls=%async_computation.1 | async-start | bytes 4718592 | tf_op jit(solution)/shard_map/psum | solution.py:71
  66.6 3.3 %copy-start.12 = (bf16[2,11,2,32,256]{4,3,2,1,0:T(8,128)(2,1)S(1)}, bf16[2,11,2,32,256]{4,3,2,1,0:T(8,128)(2,1)}, u32[]{:S(2)}) copy-start(bf16[2,11,2,32,256]{4,3,2,1,0:T(8,128)(2,1)} %get-tuple-element.6) | copy-start | bytes 2162692
  66.6 3.3 %copy-start.18 = (bf16[1408,256]{1,0:T(8,128)(2,1)S(1)}, bf16[1408,256]{1,0:T(8,128)(2,1)}, u32[]{:S(2)}) copy-start(bf16[1408,256]{1,0:T(8,128)(2,1)} %get-tuple-element.3) | copy-start | bytes 2162692
  67.6 3.4 %copy-start.10 = (bf16[2,11,2,32,256]{4,3,2,1,0:T(8,128)(2,1)S(1)}, bf16[2,11,2,32,256]{4,3,2,1,0:T(8,128)(2,1)}, u32[]{:S(2)}) copy-start(bf16[2,11,2,32,256]{4,3,2,1,0:T(8,128)(2,1)} %get-tuple-element.7) | copy-start | bytes 2162692
  69.9 2.2 copy-start.8
  72.2 2.2 copy-start.6
  73.3 2.2 copy-start.4
  75.5 2.2 copy-start.17
Sparse Core Ops, SparseCore 0:
  66.7 159.3 reduce-scatter.3
Sparse Core Ops, SparseCore 1:
  79.0 215.9 all-reduce.2
where the time goes:
time: 306 us
  waiting for transfers between devices  183 us (60%)
  blocking collectives  62.8 us (21%)
  local copies, waits for them, and re-layouts  24.7 us (8%)
  matrix products  19.2 us (6%)
  between operations  15.6 us (5%)
    unnamed x3, waiting for transfers between devices  142 us
    psum x1, waiting for transfers between devices, on_device(): conv_grad = lax.psum(taps, ('frame', 'cam'))  40.5 us
    all_gather x1, blocking collectives, on_device(): lax.all_gather(joined_grad, 'cam', axis=1, tiled=True).astype(jnp.float32)  32.4 us
    psum x1, blocking collectives, on_device(): latent = lax.psum(partial_latent, 'cam')  20.2 us
    unnamed x47, local copies, waits for them, and re-layouts  16.6 us
    dot_general x9, matrix products, on_device(): lax.dot_general(shifted[k], pre_grad, (((0,), (0,)), ((), ())), preferred...  11.2 us
  transfers between devices with their start and end apart: 2, of which 2 were waited for; matrix products, arithmetic and copies ran while one was open for 5% of the time, Pallas kernels for 0%

commit v1 on v0

--- a/solution.py
+++ b/solution.py
@@ -45,7 +45,9 @@
     ).astype(jnp.bfloat16)
     weighting = mask_f / cam_count[:, None]
     scaled = (
-        lax.all_gather(joined_grad, "cam", axis=1, tiled=True).astype(jnp.float32)[:, None, :]
+        jnp.concatenate(
+            lax.all_to_all(jnp.stack([joined_grad] * lax.axis_size("cam")), "cam", 0, 0), axis=1
+        ).astype(jnp.float32)[:, None, :]
         * weighting[:, :, None]
         * slopes
     )

time: 306 us -> 287 us (0.938)
  blocking collectives: 62.8 us -> 30.4 us
  waiting for transfers between devices: 183 us -> 193 us
  starting transfers between devices: 0.08 us -> 7.39 us
  matrix products: 19.2 us -> 15.6 us
    all_gather x1 -> x0, blocking collectives: 32.4 us -> none  [on_device(): lax.all_gather(joined_grad, 'cam', axis=1, tiled=True).astype(jnp.float32)]
    unnamed x3, waiting for transfers between devices: 142 us -> 152 us
    all_to_all x0 -> x1, starting transfers between devices: none -> 7.31 us  [on_device(): lax.all_to_all(jnp.stack([joined_grad] * lax.axis_size('cam')), 'cam', 0, 0)]
    dot_general x9, matrix products: 11.2 us -> 4.42 us  [on_device(): lax.dot_general(shifted[k], pre_grad, (((0,), (0,)), ((), ())), preferred...]
  transfers between devices with their start and end apart: 2 -> 3, of which waited for: 2 -> 2; matrix products, arithmetic and copies ran while one was open for 5% -> 4% of each run, Pallas kernels for 0% -> 0%
where the time goes in v1:
time: 287 us; the launch traced here: 286 us
  waiting for transfers between devices  193 us (67%)
  blocking collectives  30.4 us (11%)
  local copies, waits for them, and re-layouts  23.5 us (8%)
  between operations  15.8 us (6%)
  matrix products  15.6 us (5%)
  starting transfers between devices  7.39 us (3%)
    unnamed x3, waiting for transfers between devices  152 us
    psum x1, waiting for transfers between devices, on_device(): conv_grad = lax.psum(taps, ('frame', 'cam'))  40.5 us
    psum x1, blocking collectives, on_device(): latent = lax.psum(partial_latent, 'cam')  20.2 us
    unnamed x47, local copies, waits for them, and re-layouts  18 us
    dot_general x9, matrix products, on_device(): jnp.dot(shifted[k], conv_weight[k], preferred_element_type=jnp.float32)  8.53 us
    all_to_all x1, starting transfers between devices, on_device(): lax.all_to_all(jnp.stack([joined_grad] * lax.axis_size('cam')), 'cam', 0, 0)  7.31 us
  transfers between devices with their start and end apart: 3, of which 2 were waited for; matrix products, arithmetic and copies ran while one was open for 4% of the time, Pallas kernels for 0%

profile of v1, /device:TPU:0, one launch (start us, length us, event | category | flops | bytes accessed | tf_op | source)
XLA Modules:
  0.0 285.9 jit_solution(14921966231475837991)
XLA Ops:
  8.0 1.2 copy-done
  9.2 1.0 convolution_convert_fusion
  10.3 0.7 stack.41
  11.0 7.3 %all-to-all-start = ((bf16[8,2,2048]{2,1,0:T(2,128)(2,1)}), bf16[8,2,2048]{2,1,0:T(2,128)(2,1)S(1)}, u32[]{:S(2)}, u32[]{:S(2)}) async-start(bf16[8,2,2048]{2,1,0:T(2,128)(2,1)} %stack.41), calls=%async_computation | async-start | bytes 131072 | tf_op jit(solution)/shard_map/all_to_all | solution.py:49
  18.3 2.8 pad_slice_fusion
  21.3 2.1 fusion.17
  23.8 0.8 copy-done.11
  24.9 0.8 copy-done.9
  26.4 0.8 copy-done.7
  27.8 1.5 convolution_add_fusion.1
  29.7 1.4 mul.41
  31.1 3.0 %multiply_convert_fusion = (bf16[1408,256]{1,0:T(8,128)(2,1)S(1)}, bf16[1408,256]{1,0:T(8,128)(2,1)S(1)}) fusion(f32[1408,256]{1,0:T(8,128)} %mul.41, f32[1408,256]{1,0:T(8,128)} %convolution_add_fusion.1, bf16[1408,256]{1,0:T(8,128)(2,1)} %bitcast.141, bf16[9,256,256]{2,1,0:T(8,128)(2,1)} %param.6), kind=kOutput, calls=%fused_computation.17 | convolution fusion | flops 188874752 | bytes 5177344 | tf_op jit(solution)/shard_map/dot_general | solution.py:22
  34.5 0.7 copy-done.14
  35.2 0.4 fusion.7
  35.7 0.4 fusion.6
  36.4 0.4 fusion.5
  36.8 0.4 fusion.4
  38.7 0.4 fusion.1
  39.1 1.4 copy-done.16
  40.5 0.5 reshape.63
  41.4 5.0 %copy.14 = f32[16384,2]{1,0:T(8,128)} copy(f32[16384,2]{0,1:T(2,128)S(1)} %bitcast.143) | data formatting | bytes 262144
  46.4 1.0 copy-done.18
  47.5 1.1 fusion
  48.6 0.6 copy-done.19
  49.3 5.1 %all-gather.1 = bf16[4,2,256]{2,1,0:T(2,128)(2,1)S(1)} all-gather(bf16[1,2,256]{2,1,0:T(2,128)(2,1)S(1)} %bitcast.145), channel_id=1, replica_groups=mesh['frame'=4,'cam'=8] {'frame'}, dimensions={0}, use_global_device_ids=true | all-gather | bytes 5120 | tf_op jit(solution)/shard_map/all_gather | solution.py:67
  54.3 152.0 %reduce-scatter.4.cloned.1.call-done = f32[2048,2]{1,0:T(8,128)} async-done(((f32[16384,2]{1,0:T(8,128)}), f32[2048,2]{1,0:T(8,128)}) %reduce-scatter.4.cloned.1.call-update) | async-done | bytes 16400
  206.3 1.6 copy.15
  208.0 5.2 %all-gather = bf16[4,2,2048]{2,1,0:T(2,128)(2,1)S(1)} all-gather(bf16[1,2,2048]{2,1,0:T(2,128)(2,1)S(1)} %fusion.68), channel_id=1, replica_groups=mesh['frame'=4,'cam'=8] {'frame'}, dimensions={0}, use_global_device_ids=true | all-gather | bytes 40960 | tf_op jit(solution)/shard_map/all_gather | solution.py:66
  213.5 20.2 %psum.14 = f32[2,256]{1,0:T(2,128)} all-reduce(f32[2,256]{1,0:T(2,128)S(1)} %fusion.34), channel_id=1, replica_groups=mesh['frame'=4,'cam'=8] {'cam'}, use_global_device_ids=true, to_apply=%region_2.3 | all-reduce | flops 512 | bytes 4096 | tf_op jit(solution)/shard_map/psum | solution.py:42
  233.7 1.1 fusion.28
  234.7 40.5 %all-reduce.3.cloned.1.call-done = f32[9,256,256]{2,1,0:T(8,128)} async-done(((f32[9,256,256]{2,1,0:T(8,128)}), f32[9,256,256]{2,1,0:T(8,128)}) %all-reduce.3.cloned.1.call-update) | async-done | bytes 2359312 | tf_op jit(solution)/shard_map/psum | solution.py:73
  275.2 3.2 %copy.29 = f32[9,256,256]{2,1,0:T(8,128)} copy(f32[9,256,256]{2,1,0:T(8,128)} %all-reduce.3.cloned.1.call-done) | data formatting | bytes 4718592
  (59 shorter events, 5.8 us)
Async XLA Ops:
  8.0 1.2 copy-start
  8.0 10.3 %copy-start.1 = (bf16[2,11,2,32,256]{4,3,2,1,0:T(8,128)(2,1)S(1)}, bf16[2,11,2,32,256]{4,3,2,1,0:T(8,128)(2,1)}, u32[]{:S(2)}) copy-start(bf16[2,11,2,32,256]{4,3,2,1,0:T(8,128)(2,1)} %param.5) | copy-start | bytes 2162692
  11.0 18.5 %all-to-all-start = ((bf16[8,2,2048]{2,1,0:T(2,128)(2,1)}), bf16[8,2,2048]{2,1,0:T(2,128)(2,1)S(1)}, u32[]{:S(2)}, u32[]{:S(2)}) async-start(bf16[8,2,2048]{2,1,0:T(2,128)(2,1)} %stack.41), calls=%async_computation | async-start | bytes 131072 | tf_op jit(solution)/shard_map/all_to_all | solution.py:49
  18.3 188.1 %reduce-scatter.4.cloned.1.call-start = ((), (), s32[]{:S(2)}) async-start(), calls=%async_computation.3 | async-start | bytes 9437184
  18.3 2.8 copy-start.20
  21.1 6.3 %copy-start.5 = (bf16[2,11,2,32,256]{4,3,2,1,0:T(8,128)(2,1)}, bf16[2,11,2,32,256]{4,3,2,1,0:T(8,128)(2,1)S(1)}, u32[]{:S(2)}) copy-start(bf16[2,11,2,32,256]{4,3,2,1,0:T(8,128)(2,1)S(1)} %get-tuple-element.10) | copy-start | bytes 2162692
  21.1 6.7 %copy-start.3 = (bf16[2,11,2,32,256]{4,3,2,1,0:T(8,128)(2,1)}, bf16[2,11,2,32,256]{4,3,2,1,0:T(8,128)(2,1)S(1)}, u32[]{:S(2)}) copy-start(bf16[2,11,2,32,256]{4,3,2,1,0:T(8,128)(2,1)S(1)} %get-tuple-element.11) | copy-start | bytes 2162692
  21.2 2.2 copy-start.13
  21.2 2.3 copy-start.17
  23.4 1.1 copy-start.11
  24.5 1.1 copy-start.9
  26.0 1.1 copy-start.7
  31.1 3.0 %copy-start.15 = (bf16[2,11,2,32,256]{4,3,2,1,0:T(8,128)(2,1)S(1)}, bf16[2,11,2,32,256]{4,3,2,1,0:T(8,128)(2,1)}, u32[]{:S(2)}) copy-start(bf16[2,11,2,32,256]{4,3,2,1,0:T(8,128)(2,1)} %get-tuple-element.12) | copy-start | bytes 2162692
  34.1 1.1 copy-start.14
  34.1 1.5 copy-start.12
  35.2 1.2 copy-start.10
  35.6 1.2 copy-start.2
  36.4 1.2 copy-start.8
  36.8 1.2 copy-start.6
  37.5 1.2 copy-start.4
  39.1 1.4 copy-start.16
  46.4 1.1 copy-start.18
  46.4 228.8 %all-reduce.3.cloned.1.call-start = ((), (), s32[]{:S(2)}) async-start(), calls=%async_computation.2 | async-start | bytes 4718592 | tf_op jit(solution)/shard_map/psum | solution.py:73
  48.6 0.7 copy-start.19
Sparse Core Ops, SparseCore 0:
  46.5 159.7 reduce-scatter.3
Sparse Core Ops, SparseCore 1:
  53.0 222.2 all-reduce.2
